TPU v7x, 32 devices: a whole 2x2x4 slice. The times are simulated.
32 devices in a mesh: groups: 2 (over y), ctx: 4 (over z), head: 2 (over x), role: 2 (over core).
Axes of the slice: x: 2, y: 2, z: 4, core: 2. Of those that a mesh axis runs over, the one named last changes fastest.
Arguments:
- prompt_query: bfloat16 [768, 64, 192], P(('groups', 'ctx'), ('head', 'role')), parts along dimension 0, may hold values from -200 to 200
- prompt_latent: bfloat16 [768, 576], P(('groups', 'ctx')), parts along dimension 0, may hold values from -60 to 60
- block_order: int32 [8], P('groups'), parts along dimension 0, may hold values from 0 to 3, as said below
- key_up: bfloat16 [64, 128, 512], P(('head', 'role')), may hold values from -0.5 to 0.5
- value_up: bfloat16 [64, 512, 128], P(('head', 'role')), may hold values from -1.796875 to 1.796875
- out_weight: bfloat16 [8192, 7168], P(('head', 'role'), 'ctx'), may hold values from -0.0625 to 0.0625
- step_query: bfloat16 [4, 8, 64, 192], P(None, 'groups', ('head', 'role')), parts along dimension 1, may hold values from -200 to 200
- cache_latent: bfloat16 [8, 1536, 576], P('groups', 'ctx'), parts along dimension 0, may hold values from -60 to 60
- step_latent: bfloat16 [4, 8, 576], P(None, 'groups'), parts along dimension 1, may hold values from -5 to 5
- cache_length: int32 [8], P('groups'), parts along dimension 0, may hold values from 2 to 1536
- block_dest: int32 [8], P('groups'), parts along dimension 0, may hold values from 0 to 3
Outputs:
- prompt_out: bfloat16 [768, 8192], P(('groups', 'ctx'), ('head', 'role')), parts along dimension 0
- step_out: bfloat16 [4, 8, 7168], P(None, 'groups', ('ctx', 'head', 'role')), parts along dimension 1
There are 2 independent parts, one for each index of `groups`. A program takes and returns all parts, laid end to end along the dimension named above; an argument that names none is the same for every part. Nothing has to cross between parts.
Inputs may be any that keep to these rules, and one draw needn't show every extreme that they name: `block_order`: a permutation: each block position appears once.
All inputs are finite; a program needn't handle non-finite values.
Results may differ from a plain program's by a relative error of at most 0.039.
Values may be sent and summed in bfloat16 or wider, within the bound.
No kernel may reach another device: no remote copies, remote signals or barrier semaphores. Data moves between devices by JAX's collectives and lax.ppermute only.
A program may use at most 64 MiB of HBM per device.

v0:
```python
import functools
import math

import jax
import jax.numpy as jnp
from jax import lax
from jax.experimental import pallas as pl
from jax.experimental.pallas import tpu as pltpu
from jax.sharding import PartitionSpec as P


BF16 = jnp.bfloat16
F32 = jnp.float32
LANES = 128
HIDDEN = -1e30
FLOOR = -1e29
TINY = 1e-30
MIB = 1 << 20

VMEM = pl.BlockSpec(memory_space=pltpu.VMEM)
ANY = pl.BlockSpec(memory_space=pl.ANY)
NT = (((1,), (1,)), ((), ()))


def dot(left, right):
    return jnp.dot(left, right, preferred_element_type=F32)


def dot_nt(left, right):
    return lax.dot_general(left, right, NT, preferred_element_type=F32)


def doublings(size):
    steps = []
    step = 1
    while step < size:
        steps.append(step)
        step *= 2
    assert step == size
    return steps


def swap(value, axis, step):
    size = lax.axis_size(axis)
    return lax.ppermute(value, axis, [(i, i ^ step) for i in range(size)])


def in_hbm(value):
    return pltpu.with_memory_space_constraint(value, pltpu.HBM)


def in_vmem(value):
    return pltpu.with_memory_space_constraint(value, pltpu.VMEM)


def params(mib):
    return pltpu.CompilerParams(vmem_limit_bytes=mib * MIB)


def split_three(value):
    high = value.astype(BF16).astype(F32)
    rest = value - high
    middle = rest.astype(BF16).astype(F32)
    return high, middle, (rest - middle).astype(BF16).astype(F32)


def pick_piece(pieces, piece_ids):
    picked = pieces[-1]
    for index in reversed(range(len(pieces) - 1)):
        picked = jnp.where(piece_ids == index, pieces[index], picked)
    return picked


def step_kernel(
    rate,
    order_hbm,
    length_hbm,
    dest_hbm,
    query_hbm,
    key_up_hbm,
    cache_hbm,
    latent_hbm,
    fresh_hbm,
    value_up_hbm,
    prompt_hbm,
    out_ref,
    key_up_ref,
    value_up_ref,
    latent_ref,
    half_ref,
    prompt_ref,
    key_pos_ref,
    query_pos_ref,
    order_ref,
    length_ref,
    dest_ref,
    query_ref,
    cache_ref,
    fresh_ref,
    nope_ref,
    row_ref,
    extra_ref,
    mixed_ref,
    sems,
):
    steps, requests, heads, width = query_ref.shape
    nope, latent = key_up_ref.shape[1:]
    span = cache_ref.shape[2]
    tokens = latent_ref.shape[0]
    pairs = steps * requests
    rows = pairs * heads
    block = steps * heads
    place = lax.axis_index("ctx")

    copies = []

    def fetch(source, target):
        copies.append(pltpu.make_async_copy(source, target, sems.at[len(copies)]))
        copies[-1].start()
        return copies[-1]

    query_copy = fetch(query_hbm, query_ref)
    chunk = heads // 2
    key_up_copies = [
        fetch(key_up_hbm.at[at : at + chunk], key_up_ref.at[at : at + chunk])
        for at in range(0, heads, chunk)
    ]
    latent_copy = fetch(latent_hbm, latent_ref)
    fresh_copy = fetch(fresh_hbm, fresh_ref)
    scalar_copies = [
        fetch(length_hbm, length_ref),
        fetch(dest_hbm, dest_ref),
        fetch(order_hbm, order_ref),
    ]
    cache_copy = fetch(cache_hbm, cache_ref)

    query_copy.wait()
    query = query_ref[...].astype(F32)
    query = jnp.concatenate(
        [query[:, request].reshape(block, width) for request in range(requests)], axis=0
    )
    nope_ref[...] = query[:, :nope]
    rope = query[:, nope:]
    for head in range(heads):
        if head % chunk == 0:
            key_up_copies[head // chunk].wait()
        part = nope_ref[pl.ds(head, pairs, stride=heads), :].astype(BF16)
        lifted = dot(part, key_up_ref[head]).astype(BF16).astype(F32)
        for lane in range(0, latent, LANES):
            row_ref[lane // LANES, pl.ds(head, pairs, stride=heads), :] = lifted[
                :, lane : lane + LANES
            ]
    value_up_copy = fetch(value_up_hbm, value_up_ref)
    prompt_copy = fetch(prompt_hbm, prompt_ref)
    row_parts = [row_ref[index] for index in range(latent // LANES)] + [rope]
    query_rows = jnp.concatenate(row_parts, axis=1).astype(BF16)

    latent_copy.wait()
    fresh_copy.wait()
    half = half_ref.shape[0]
    for index in range(2):

        @pl.when(lax.axis_index("role") == index)
        def _():
            half_ref[...] = latent_ref[index * half : (index + 1) * half, :]

    extra_ref[:tokens, :] = latent_ref[...].astype(F32)
    for step in range(steps):
        extra_ref[tokens + step * requests : tokens + (step + 1) * requests, :] = fresh_ref[
            step
        ].astype(F32)
    extra = extra_ref[...].astype(BF16)
    more = dot_nt(query_rows, extra)
    for copy in scalar_copies:
        copy.wait()
    column = lax.broadcasted_iota(jnp.int32, more.shape, 1)
    row = lax.broadcasted_iota(jnp.int32, more.shape, 0)
    fresh_id = column - tokens
    seen = ((column < tokens) & (row // block == dest_ref[place])) | (
        (column >= tokens)
        & (fresh_id % requests == row // block)
        & (fresh_id // requests <= row // heads % steps)
        & (place == 0)
    )
    more = jnp.where(seen, more, HIDDEN)
    position = place * span + lax.broadcasted_iota(jnp.int32, (1, span), 1)
    cache_copy.wait()
    scores = [
        jnp.where(
            position < length_ref[request],
            dot(query_rows[request * block : (request + 1) * block], cache_ref[request]),
            HIDDEN,
        )
        for request in range(requests)
    ]
    scores = jnp.concatenate(scores, axis=0)
    high = jnp.maximum(
        jnp.max(scores, axis=1, keepdims=True), jnp.max(more, axis=1, keepdims=True)
    )
    high = jnp.maximum(high, FLOOR)
    weights = jnp.exp2((scores - high) * rate)
    more = jnp.exp2((more - high) * rate)
    total = jnp.sum(weights, axis=1, keepdims=True) + jnp.sum(more, axis=1, keepdims=True)
    weights = weights.astype(BF16)
    mixed = jnp.concatenate(
        [
            dot_nt(weights[request * block : (request + 1) * block], cache_ref[request, :latent])
            for request in range(requests)
        ],
        axis=0,
    )
    mixed = mixed + dot(more.astype(BF16), extra[:, :latent])
    mixed = mixed * (1.0 / jnp.maximum(total, TINY))
    for lane in range(0, latent, LANES):
        mixed_ref[lane // LANES] = mixed[:, lane : lane + LANES]
    high = jnp.broadcast_to(high, (rows, LANES))
    total = jnp.broadcast_to(total, (rows, LANES))

    value_up_copy.wait()
    value_width = value_up_ref.shape[2]
    for head in range(heads):
        parts = [
            mixed_ref[index, pl.ds(head, pairs, stride=heads), :]
            for index in range(latent // LANES)
        ]
        part = jnp.concatenate(parts, axis=1).astype(BF16)
        out_ref[:, head * value_width : (head + 1) * value_width] = dot(
            part, value_up_ref[head]
        ).astype(BF16)
    lane = lax.broadcasted_iota(jnp.int32, (rows, LANES), 1)
    head_of_row = lax.broadcasted_iota(jnp.int32, (rows, LANES), 0) % heads
    pieces = split_three(high) + split_three(total)
    packed = pick_piece(pieces, lane // heads)
    packed = jnp.where((lane % heads == head_of_row) & (lane < 6 * heads), packed, 0.0)
    packed = jnp.sum(packed.reshape(pairs, heads, LANES), axis=1)
    out_ref[:, heads * value_width :] = packed.astype(BF16)

    key_id = lax.broadcasted_iota(jnp.int32, key_pos_ref.shape, 1)
    base = key_id
    for slot in range(key_pos_ref.shape[1] // tokens):
        move = (order_ref[place ^ slot] - slot) * tokens
        base = base + jnp.where(key_id // tokens == slot, move, 0)
    key_pos_ref[...] = base
    query_pos_ref[...] = order_ref[place] * tokens + lax.broadcasted_iota(
        jnp.int32, query_pos_ref.shape, 0
    )
    prompt_copy.wait()


def step_part(
    rate,
    block_order,
    cache_length,
    block_dest,
    step_query,
    key_up,
    cache,
    latent,
    fresh,
    value_up,
    prompt_query,
):
    steps, requests, heads, _ = step_query.shape
    nope, latent_width = key_up.shape[1:]
    full = cache.shape[1]
    tokens = latent.shape[0]
    pairs = steps * requests
    rows = pairs * heads
    shape = pltpu.VMEM
    return pl.pallas_call(
        functools.partial(step_kernel, rate),
        out_shape=(
            shape((pairs, heads * value_up.shape[2] + LANES), BF16),
            shape(key_up.shape, BF16),
            shape(value_up.shape, BF16),
            shape(latent.shape, BF16),
            shape((tokens // 2, full), BF16),
            shape(prompt_query.shape, BF16),
            shape((8, tokens * lax.axis_size("ctx")), jnp.int32),
            shape((tokens, LANES), jnp.int32),
        ),
        in_specs=[ANY] * 10,
        out_specs=[VMEM] * 8,
        scratch_shapes=[
            pltpu.SMEM(block_order.shape, jnp.int32),
            pltpu.SMEM(cache_length.shape, jnp.int32),
            pltpu.SMEM(block_dest.shape, jnp.int32),
            pltpu.VMEM(step_query.shape, BF16),
            pltpu.VMEM(cache.shape, BF16),
            pltpu.VMEM(fresh.shape, BF16),
            pltpu.VMEM((rows, nope), F32),
            pltpu.VMEM((latent_width // LANES, rows, LANES), F32),
            pltpu.VMEM((tokens + pairs, full), F32),
            pltpu.VMEM((latent_width // LANES, rows, LANES), F32),
            pltpu.SemaphoreType.DMA((11,)),
        ],
        compiler_params=params(16),
        cost_estimate=pl.CostEstimate(flops=10**9, bytes_accessed=10**7, transcendentals=10**5),
        name="step_part",
    )(
        *(
            in_hbm(value)
            for value in (
                block_order,
                cache_length,
                block_dest,
                step_query,
                key_up,
                cache,
                latent,
                fresh,
                value_up,
                prompt_query,
            )
        )
    )


def read_stats(packed, heads):
    def piece(index):
        if index == 0:
            return packed
        return pltpu.roll(packed, LANES - index * heads, 1)

    return piece(0) + piece(1) + piece(2), piece(3) + piece(4) + piece(5)


def merge(rate, first_ref, second_ref, heads):
    split = first_ref.shape[1] - LANES
    value_width = split // heads
    high_a, total_a = read_stats(first_ref[:, split:].astype(F32), heads)
    high_b, total_b = read_stats(second_ref[:, split:].astype(F32), heads)
    high = jnp.maximum(high_a, high_b)
    share_a = total_a * jnp.exp2((high_a - high) * rate)
    share_b = total_b * jnp.exp2((high_b - high) * rate)
    total = share_a + share_b
    inverse = 1.0 / jnp.maximum(total, TINY)
    share_a = share_a * inverse
    share_b = share_b * inverse
    merged = []
    for head in range(heads):
        at = slice(head * value_width, (head + 1) * value_width)
        merged.append(
            (
                first_ref[:, at].astype(F32) * share_a[:, head : head + 1]
                + second_ref[:, at].astype(F32) * share_b[:, head : head + 1]
            ).astype(BF16)
        )
    return merged, high, total


def merge_kernel(rate, heads, first_ref, second_ref, out_ref):
    merged, high, total = merge(rate, first_ref, second_ref, heads)
    value_width = merged[0].shape[1]
    for head in range(heads):
        out_ref[:, head * value_width : (head + 1) * value_width] = merged[head]
    pieces = split_three(high) + split_three(total)
    lane = lax.broadcasted_iota(jnp.int32, high.shape, 1)
    moved = [p if i == 0 else pltpu.roll(p, i * heads, 1) for i, p in enumerate(pieces)]
    packed = jnp.where(lane < 6 * heads, pick_piece(moved, lane // heads), 0.0)
    out_ref[:, heads * value_width :] = packed.astype(BF16)


def merge_parts(rate, heads, first, second):
    return pl.pallas_call(
        functools.partial(merge_kernel, rate, heads),
        out_shape=pltpu.VMEM(first.shape, BF16),
        in_specs=[VMEM] * 2,
        out_specs=VMEM,
        compiler_params=params(2),
        cost_estimate=pl.CostEstimate(
            flops=8 * 10**9, bytes_accessed=2 * 10**5, transcendentals=10**4
        ),
        name="merge_parts",
    )(in_vmem(first), in_vmem(second))


def join_kernel(first_ref, second_ref, out_ref):
    rows = first_ref.shape[0]
    out_ref[:rows, :] = first_ref[...]
    out_ref[rows:, :] = second_ref[...]


def gather_kernel(own_ref, mine_ref, other_ref, out_ref):
    tokens = own_ref.shape[0]
    half = tokens // 2
    out_ref[:tokens, :] = own_ref[...]
    for index, sources in enumerate(((mine_ref, other_ref), (other_ref, mine_ref))):

        @pl.when(lax.axis_index("role") == index)
        def _():
            for part, source in enumerate(sources):
                for place, slot in enumerate((2, 1, 3)):
                    at = slot * tokens + part * half
                    out_ref[at : at + half, :] = source[place * half : (place + 1) * half, :]


def half_kernel(keys_ref, out_ref):
    rows = out_ref.shape[0]
    for index in range(2):

        @pl.when(lax.axis_index("role") == index)
        def _():
            out_ref[...] = keys_ref[index * rows : (index + 1) * rows, :]


def extend_kernel(keys_ref, mine_ref, other_ref, out_ref):
    rows = keys_ref.shape[0]
    half = mine_ref.shape[0]
    out_ref[:rows, :] = keys_ref[...]
    for index, sources in enumerate(((mine_ref, other_ref), (other_ref, mine_ref))):

        @pl.when(lax.axis_index("role") == index)
        def _():
            out_ref[rows : rows + half, :] = sources[0][...]
            out_ref[rows + half :, :] = sources[1][...]


def move_rows(body, rows, *sources):
    return pl.pallas_call(
        body,
        out_shape=pltpu.VMEM((rows, sources[0].shape[1]), BF16),
        in_specs=[VMEM] * len(sources),
        out_specs=VMEM,
        compiler_params=params(1),
        cost_estimate=pl.CostEstimate(flops=10**4, bytes_accessed=4 * 10**5, transcendentals=0),
    )(*(in_vmem(source) for source in sources))


def finish_kernel(
    rate, heads, parts, first_ref, second_ref, weight_ref, keep_ref, give_ref
):
    merged, _, _ = merge(rate, first_ref, second_ref, heads)
    chunk = heads // 2
    size = chunk * merged[0].shape[1]
    product = 0.0
    for index in range(2):
        rows = jnp.concatenate(merged[index * chunk : (index + 1) * chunk], axis=1)
        product = product + dot(rows, weight_ref[index * size : (index + 1) * size, :])
    width = product.shape[1] // parts
    upper = lax.axis_index("role") == 1
    for index in range(parts // 2):
        low, high = (
            product[:, part * width : (part + 1) * width] for part in (2 * index, 2 * index + 1)
        )
        keep_ref[index] = jnp.where(upper, high, low)
        give_ref[index] = jnp.where(upper, low, high).astype(BF16)


def finish_steps(rate, heads, parts, first, second, weight):
    pairs = first.shape[0]
    shape = (parts // 2, pairs, weight.shape[1] // parts)
    return pl.pallas_call(
        functools.partial(finish_kernel, rate, heads, parts),
        out_shape=(pltpu.VMEM(shape, F32), pltpu.VMEM(shape, BF16)),
        in_specs=[VMEM] * 3,
        out_specs=[VMEM] * 2,
        compiler_params=params(4),
        cost_estimate=pl.CostEstimate(
            flops=5 * 10**8, bytes_accessed=8 * 10**6, transcendentals=10**4
        ),
        name="finish_steps",
    )(*(in_vmem(v) for v in (first, second, weight)))


def fold_kernel(step, keep_ref, received_ref, new_keep_ref, give_ref):
    share = keep_ref[...] + received_ref[...].astype(F32)
    middle = share.shape[0] // 2
    upper = lax.axis_index("head") & step != 0
    new_keep_ref[...] = jnp.where(upper, share[middle:], share[:middle])
    give_ref[...] = jnp.where(upper, share[:middle], share[middle:]).astype(BF16)


def fold_steps(step, keep, received):
    shape = (keep.shape[0] // 2, *keep.shape[1:])
    return pl.pallas_call(
        functools.partial(fold_kernel, step),
        out_shape=(pltpu.VMEM(shape, F32), pltpu.VMEM(shape, BF16)),
        in_specs=[VMEM] * 2,
        out_specs=[VMEM] * 2,
        compiler_params=params(1),
        cost_estimate=pl.CostEstimate(flops=10**5, bytes_accessed=10**5, transcendentals=0),
        name="fold_steps",
    )(in_vmem(keep), in_vmem(received))


def lift_kernel(heads, query_ref, key_up_ref, row_ref, nope_ref, rope_ref):
    tokens, every, width = query_ref.shape
    nope, latent = key_up_ref.shape[1:]
    nope_ref[...] = query_ref[:, :, :nope].astype(F32).reshape(tokens * every, nope)
    rope_ref[:, : width - nope] = (
        query_ref[:, :, nope:].astype(F32).reshape(tokens * every, width - nope)
    )
    for index, head in enumerate(heads):
        at = slice(index * tokens, (index + 1) * tokens)
        part = nope_ref[pl.ds(head, tokens, stride=every), :].astype(BF16)
        row_ref[at, :latent] = dot(part, key_up_ref[head]).astype(BF16)
        rope = rope_ref[pl.ds(head, tokens, stride=every), :]
        row_ref[at, latent:] = rope[:, : width - nope].astype(BF16)


def prompt_lift(heads, prompt_query, key_up):
    tokens, every, width = prompt_query.shape
    nope, latent_width = key_up.shape[1:]
    return pl.pallas_call(
        functools.partial(lift_kernel, heads),
        out_shape=pltpu.VMEM((tokens * len(heads), latent_width + width - nope), BF16),
        in_specs=[VMEM] * 2,
        out_specs=VMEM,
        scratch_shapes=[
            pltpu.VMEM((tokens * every, nope), F32),
            pltpu.VMEM((tokens * every, LANES), F32),
        ],
        compiler_params=params(8),
        cost_estimate=pl.CostEstimate(
            flops=8 * 10**8, bytes_accessed=3 * 10**6, transcendentals=0
        ),
        name="prompt_lift",
    )(in_vmem(prompt_query), in_vmem(key_up))


def attend(
    rate, group, heads, row_refs, key_ref, key_pos_ref, query_pos_ref, value_up_ref, put
):
    tokens = query_pos_ref.shape[0]
    count = key_ref.shape[0]
    latent = value_up_ref.shape[1]
    visible = (key_pos_ref[:1, :] <= query_pos_ref[:, :1])[None]

    def score(first):
        first = first * tokens
        for rows in row_refs:
            if first < rows.shape[0]:
                return dot_nt(rows[first : first + group * tokens, :], key_ref[...])
            first -= rows.shape[0]

    firsts = list(range(heads.start, heads.stop, group))
    ahead = score(firsts[0])
    for first in firsts:
        scores = ahead
        if first != firsts[-1]:
            ahead = score(first + group)
        scores = jnp.where(visible, scores.reshape(group, tokens, count), HIDDEN)
        scores = scores.reshape(group * tokens, count)
        weights = jnp.exp2((scores - jnp.max(scores, axis=1, keepdims=True)) * rate)
        inverse = 1.0 / jnp.sum(weights, axis=1, keepdims=True)
        mixed = dot(weights.astype(BF16), key_ref[:, :latent]).astype(BF16)
        for index in range(group):
            part = slice(index * tokens, (index + 1) * tokens)
            value = dot(mixed[part], value_up_ref[first + index]) * inverse[part]
            put(first + index, value.astype(BF16))


def front_kernel(
    rate,
    group,
    heads,
    early_ref,
    late_ref,
    key_ref,
    key_pos_ref,
    query_pos_ref,
    value_up_ref,
    out_ref,
):
    width = value_up_ref.shape[2]

    def put(head, value):
        at = (head - heads.start) * width
        out_ref[:, at : at + width] = value

    attend(
        rate,
        group,
        heads,
        (early_ref, late_ref),
        key_ref,
        key_pos_ref,
        query_pos_ref,
        value_up_ref,
        put,
    )


def prompt_front(rate, group, heads, rows, keys, key_pos, query_pos, value_up):
    tokens = query_pos.shape[0]
    return pl.pallas_call(
        functools.partial(front_kernel, rate, group, heads),
        out_shape=pltpu.VMEM((tokens, len(heads) * value_up.shape[2]), BF16),
        in_specs=[VMEM] * 6,
        out_specs=VMEM,
        compiler_params=params(16),
        cost_estimate=pl.CostEstimate(
            flops=4 * 10**8, bytes_accessed=3 * 10**6, transcendentals=3 * 10**5
        ),
        name="prompt_front",
    )(*(in_vmem(v) for v in (*rows, keys, key_pos, query_pos, value_up)))


def back_kernel(
    rate,
    group,
    heads,
    early_ref,
    late_ref,
    key_ref,
    key_pos_ref,
    query_pos_ref,
    value_up_ref,
    front_ref,
    keep_ref,
    received_ref,
    out_hbm,
    steps_hbm,
    back_ref,
    steps_ref,
    sems,
):
    width = value_up_ref.shape[2]
    edge = heads.start * width
    copies = []

    def send(source, target):
        copies.append(pltpu.make_async_copy(source, target, sems.at[len(copies)]))
        copies[-1].start()

    send(front_ref, out_hbm.at[:, :edge])
    share = keep_ref[0] + received_ref[0].astype(F32)
    steps, requests, _ = steps_ref.shape
    for step in range(steps):
        rows = [share[at : at + 1] for at in range(step, steps * requests, steps)]
        steps_ref[step] = jnp.concatenate(rows, axis=0).astype(BF16)
    send(steps_ref, steps_hbm)

    def put(head, value):
        at = (head - heads.start) * width
        back_ref[:, at : at + width] = value
        if (head - heads.start + 1) % group == 0:
            start = at + width - group * width
            send(
                back_ref.at[:, start : at + width],
                out_hbm.at[:, edge + start : edge + at + width],
            )

    attend(
        rate,
        group,
        heads,
        (early_ref, late_ref),
        key_ref,
        key_pos_ref,
        query_pos_ref,
        value_up_ref,
        put,
    )
    for copy in copies:
        copy.wait()


def prompt_back(
    rate, group, heads, steps, rows, keys, key_pos, query_pos, value_up, front, keep, received
):
    tokens = query_pos.shape[0]
    width = value_up.shape[2]
    pairs, columns = keep.shape[1:]
    step_shape = (steps, pairs // steps, columns)
    return pl.pallas_call(
        functools.partial(back_kernel, rate, group, heads),
        out_shape=(
            jax.ShapeDtypeStruct((tokens, heads.stop * width), BF16),
            jax.ShapeDtypeStruct(step_shape, BF16),
        ),
        in_specs=[VMEM] * 9,
        out_specs=[ANY] * 2,
        scratch_shapes=[
            pltpu.VMEM((tokens, len(heads) * width), BF16),
            pltpu.VMEM(step_shape, BF16),
            pltpu.SemaphoreType.DMA((2 + len(heads) // group,)),
        ],
        compiler_params=params(16),
        cost_estimate=pl.CostEstimate(
            flops=8 * 10**8, bytes_accessed=6 * 10**6, transcendentals=3 * 10**5
        ),
        name="prompt_back",
    )(
        *(
            in_vmem(v)
            for v in (*rows, keys, key_pos, query_pos, value_up, front, keep, received)
        )
    )


def per_device(
    prompt_query,
    prompt_latent,
    block_order,
    key_up,
    value_up,
    out_weight,
    step_query,
    cache_latent,
    step_latent,
    cache_length,
    block_dest,
):
    heads, width = prompt_query.shape[1:]
    rate = width ** (-0.5) * math.log2(math.e)
    context_size = lax.axis_size("ctx")
    steps = step_query.shape[0]
    head_size = lax.axis_size("head")
    role_size = lax.axis_size("role")

    rounds = doublings(context_size)
    assert role_size == 2 and context_size >= 4
    (
        running,
        key_up,
        value_up,
        latent,
        half,
        prompt_query,
        key_pos,
        query_pos,
    ) = step_part(
        rate,
        block_order,
        cache_length,
        block_dest,
        step_query,
        key_up,
        jnp.swapaxes(cache_latent, 1, 2),
        prompt_latent,
        step_latent,
        value_up,
        prompt_query,
    )
    edge = heads - heads // 4
    early = edge // 2
    early_rows = prompt_lift(range(early), prompt_query, key_up)
    late_rows = prompt_lift(range(early, heads), prompt_query, key_up)
    rows = (early_rows, late_rows)
    for step in rounds:
        far_running = swap(running, "ctx", step)
        if step != rounds[-1]:
            running = merge_parts(rate, heads, running, far_running)
    far = swap(half, "ctx", 2)
    near = swap(move_rows(join_kernel, 2 * half.shape[0], half, far), "ctx", 1)
    mine = move_rows(join_kernel, 3 * half.shape[0], far, near)
    other = swap(mine, "role", 1)
    keys = move_rows(gather_kernel, 4 * latent.shape[0], latent, mine, other)
    for step in rounds[2:]:
        sent = move_rows(half_kernel, keys.shape[0] // 2, keys)
        received = swap(sent, "ctx", step)
        keys = move_rows(
            extend_kernel, 2 * keys.shape[0], keys, received, swap(received, "role", 1)
        )
    front = prompt_front(rate, early, range(edge), rows, keys, key_pos, query_pos, value_up)
    keep, give = finish_steps(
        rate, heads, head_size * role_size, running, far_running, out_weight
    )
    partial = swap(give, "role", 1)
    for step in reversed(doublings(head_size)):
        keep, give = fold_steps(step, keep, partial)
        partial = swap(give, "head", step)
    return prompt_back(
        rate,
        heads - edge,
        range(edge, heads),
        steps,
        rows,
        keys,
        key_pos,
        query_pos,
        value_up,
        front,
        keep,
        partial,
    )


def solution(mesh):
    return jax.shard_map(
        per_device,
        mesh=mesh,
        in_specs=(
            P(("groups", "ctx"), ("head", "role"), None),
            P(("groups", "ctx"), None),
            P("groups"),
            P(("head", "role"), None, None),
            P(("head", "role"), None, None),
            P(("head", "role"), "ctx"),
            P(None, "groups", ("head", "role"), None),
            P("groups", "ctx", None),
            P(None, "groups", None),
            P("groups"),
            P("groups"),
        ),
        out_specs=(
            P(("groups", "ctx"), ("head", "role")),
            P(None, "groups", ("ctx", "head", "role")),
        ),
        check_vma=False,
    )
```

profile of v0, /device:TPU:0, one launch (start us, length us, event | category | flops | bytes accessed | tf_op | source)
XLA Modules:
  0.0 27.9 jit_solution(713811390455270006)
XLA Ops:
  0.6 4.1 %step_part.1 = (bf16[16,2176]{1,0:T(8,128)(2,1)S(1)}, bf16[16,128,512]{2,1,0:T(8,128)(2,1)S(1)}, bf16[16,512,128]{2,1,0:T(8,128)(2,1)S(1)}, bf16[96,576]{1,0:T(8...) custom-call(s32[4]{0:T(128)} %order_hbm.1, ...), custom_call_target="tpu_custom_call" | custom-call | flops 1000000000 | bytes 10000000 | tf_op jit(solution)/shard_map/step_part/pallas_call | solution.py:270
  4.8 3.1 %collective-permute-start.3 = (bf16[16,2176]{1,0:T(8,128)(2,1)S(1)}, bf16[16,2176]{1,0:T(8,128)(2,1)S(1)}, u32[]{:S(2)}, u32[]{:S(2)}) collective-permute-start(bf16[16,2176]{1,0:T(8,128)(2,1)S(1)} %get-tuple-element.21.first_ref), channel_id=1, source_target_pairs={{0,4},{4,0},{8,12},{12,8},{1,5},{5,1},{9,13},{13,9},{2,6},{6,2},{1... | collective-permute-start | bytes 208904 | tf_op jit(solution)/shard_map/ppermute | solution.py:45
  7.9 2.6 %collective-permute-start = (bf16[48,576]{1,0:T(8,128)(2,1)S(1)}, bf16[48,576]{1,0:T(8,128)(2,1)S(1)}, u32[]{:S(2)}, u32[]{:S(2)}) collective-permute-start(bf16[48,576]{1,0:T(8,128)(2,1)S(1)} %get-tuple-element.17.first_ref), channel_id=1, source_target_pairs={{0,8},{4,12},{8,0},{12,4},{1,9},{5,13},{9,1},{13,5},{2,10},{6,14},... | collective-permute-start | bytes 165896 | tf_op jit(solution)/shard_map/ppermute | solution.py:45
  10.5 3.2 %collective-permute-done.second_ref.first_ref = bf16[48,576]{1,0:T(8,128)(2,1)S(1)} collective-permute-done((bf16[48,576]{1,0:T(8,128)(2,1)S(1)}, bf16[48,576]{1,0:T(8,128)(2,1)S(1)}, u32[]{:S(2)}, u32[]{:S(2)}) %collective-permute-start) | collective-permute-done | bytes 55328 | tf_op jit(solution)/shard_map/ppermute | solution.py:45
  13.7 0.0 slice-start
  13.7 0.0 slice-start.1
  13.7 0.6 %collective-permute-start.1 = (bf16[96,576]{1,0:T(8,128)(2,1)S(1)}, bf16[96,576]{1,0:T(8,128)(2,1)S(1)}, u32[]{:S(2)}, u32[]{:S(2)}) collective-permute-start(bf16[96,576]{1,0:T(8,128)(2,1)S(1)} %shard_map.122), channel_id=1, source_target_pairs={{0,4},{4,0},{8,12},{12,8},{1,5},{5,1},{9,13},{13,9},{2,6},{6,2},{1... | collective-permute-start | bytes 331784 | tf_op jit(solution)/shard_map/ppermute | solution.py:45
  14.3 0.0 collective-permute-done.3.second_ref
  14.3 0.3 merge_parts.1.first_ref
  14.6 2.1 %collective-permute-start.4 = (bf16[16,2176]{1,0:T(8,128)(2,1)S(1)}, bf16[16,2176]{1,0:T(8,128)(2,1)S(1)}, u32[]{:S(2)}, u32[]{:S(2)}) collective-permute-start(bf16[16,2176]{1,0:T(8,128)(2,1)S(1)} %merge_parts.1.first_ref), channel_id=1, source_target_pairs={{0,8},{4,12},{8,0},{12,4},{1,9},{5,13},{9,1},{13,5},{2,10},{6,14},... | collective-permute-start | bytes 208904 | tf_op jit(solution)/shard_map/ppermute | solution.py:45
  16.7 2.0 %collective-permute-done.1.second_ref = bf16[96,576]{1,0:T(8,128)(2,1)S(1)} collective-permute-done((bf16[96,576]{1,0:T(8,128)(2,1)S(1)}, bf16[96,576]{1,0:T(8,128)(2,1)S(1)}, u32[]{:S(2)}, u32[]{:S(2)}) %collective-permute-start.1) | collective-permute-done | bytes 110624 | tf_op jit(solution)/shard_map/ppermute | solution.py:45
  18.7 0.1 collective-permute-start.2
  18.8 0.5 %prompt_lift.2.early_ref = bf16[576,576]{1,0:T(8,128)(2,1)S(1)} custom-call(bf16[96,16,192]{2,1,0:T(8,128)(2,1)S(1)} %get-tuple-element.14.query_ref, bf16[16,128,512]{2,1,0:T(8,128)(2,1)S(1)} %get-tuple-element.15.key_up_ref), custom_call_target="tpu_custom_call" | custom-call | flops 800000000 | bytes 3000000 | tf_op jit(solution)/shard_map/prompt_lift/pallas_call | solution.py:505
  19.3 0.6 %collective-permute-done.4.second_ref = bf16[16,2176]{1,0:T(8,128)(2,1)S(1)} collective-permute-done((bf16[16,2176]{1,0:T(8,128)(2,1)S(1)}, bf16[16,2176]{1,0:T(8,128)(2,1)S(1)}, u32[]{:S(2)}, u32[]{:S(2)}) %collective-permute-start.4) | collective-permute-done | bytes 69664 | tf_op jit(solution)/shard_map/ppermute | solution.py:45
  19.9 0.0 slice-done
  19.9 0.0 slice-done.1
  19.9 1.3 %finish_steps.1 = (f32[2,16,448]{2,1,0:T(8,128)S(1)}, bf16[2,16,448]{2,1,0:T(8,128)(2,1)S(1)}) custom-call(bf16[16,2176]{1,0:T(8,128)(2,1)S(1)} %merge_parts.1.first_ref, bf16[16,2176]{1,0:T(8,128)(2,1)S(1)} %collective-permute-done.4.second_ref, bf16[2048,1792]{1,0:T(8,128)(2,1)S(1)} %bitcast.2), custom_call_target="tpu_custom_call" | custom-call | flops 500000000 | bytes 8000000 | tf_op jit(solution)/shard_map/finish_steps/pallas_call | solution.py:453
  21.2 0.0 collective-permute-start.5
  21.3 0.8 %prompt_lift.3.late_ref = bf16[960,576]{1,0:T(8,128)(2,1)S(1)} custom-call(bf16[96,16,192]{2,1,0:T(8,128)(2,1)S(1)} %get-tuple-element.14.query_ref, bf16[16,128,512]{2,1,0:T(8,128)(2,1)S(1)} %get-tuple-element.15.key_up_ref), custom_call_target="tpu_custom_call" | custom-call | flops 800000000 | bytes 3000000 | tf_op jit(solution)/shard_map/prompt_lift/pallas_call | solution.py:505
  22.1 0.4 %collective-permute-done.5.received_ref = bf16[2,16,448]{2,1,0:T(8,128)(2,1)S(1)} collective-permute-done((bf16[2,16,448]{2,1,0:T(8,128)(2,1)S(1)}, bf16[2,16,448]{2,1,0:T(8,128)(2,1)S(1)}, u32[]{:S(2)}, u32[]{:S(2)}) %collective-permute-start.5) | collective-permute-done | bytes 28704 | tf_op jit(solution)/shard_map/ppermute | solution.py:45
  22.5 1.6 %collective-permute-start.6 = (bf16[1,16,448]{2,1,0:T(8,128)(2,1)S(1)}, bf16[1,16,448]{2,1,0:T(8,128)(2,1)S(1)}, u32[]{:S(2)}, u32[]{:S(2)}) collective-permute-start(bf16[1,16,448]{2,1,0:T(8,128)(2,1)S(1)} %get-tuple-element.25), channel_id=1, source_target_pairs={{0,2},{2,0},{1,3},{3,1},{4,6},{6,4},{5,7},{7,5},{8,10},{10,8},{9,1... | collective-permute-start | bytes 43016 | tf_op jit(solution)/shard_map/ppermute | solution.py:45
  24.0 0.0 collective-permute-done.2.other_ref
  24.1 2.1 %prompt_front.1.front_ref = bf16[96,1536]{1,0:T(8,128)(2,1)S(1)} custom-call(bf16[576,576]{1,0:T(8,128)(2,1)S(1)} %prompt_lift.2.early_ref, bf16[960,576]{1,0:T(8,128)(2,1)S(1)} %prompt_lift.3.late_ref, bf16[384,576]{1,0:T(8,128)(2,1)S(1)} %shard_map.124.key_ref, s32[8,384]{1,0:T(8,128)S(1)} %get-tuple-element.18.key_pos_ref, ...), custom_call_target="tpu_custom_call" | custom-call | flops 400000000 | bytes 3000000 | tf_op jit(solution)/shard_map/prompt_front/pallas_call | solution.py:587
  26.2 0.1 collective-permute-done.6.received_ref
  26.3 1.7 %prompt_back.1 = (bf16[96,2048]{1,0:T(8,128)(2,1)}, bf16[4,4,448]{2,1,0:T(4,128)(2,1)}) custom-call(bf16[576,576]{1,0:T(8,128)(2,1)S(1)} %prompt_lift.2.early_ref, bf16[960,576]{1,0:T(8,128)(2,1)S(1)} %prompt_lift.3.late_ref, bf16[384,576]{1,0:T(8,128)(2,1)S(1)} %shard_map.124.key_ref, s32[8,384]{1,0:T(8,128)S(1)} %get-tuple-element.18.key_pos_ref, ...), custom_call_target="tpu_custom_call" | custom-call | flops 800000000 | bytes 6000000 | tf_op jit(solution)/shard_map/prompt_back/pallas_call | solution.py:667
  (5 shorter events, 0.1 us)
Async XLA Ops:
  4.8 9.6 %collective-permute-start.3 = (bf16[16,2176]{1,0:T(8,128)(2,1)S(1)}, bf16[16,2176]{1,0:T(8,128)(2,1)S(1)}, u32[]{:S(2)}, u32[]{:S(2)}) collective-permute-start(bf16[16,2176]{1,0:T(8,128)(2,1)S(1)} %get-tuple-element.21.first_ref), channel_id=1, source_target_pairs={{0,4},{4,0},{8,12},{12,8},{1,5},{5,1},{9,13},{13,9},{2,6},{6,2},{1... | collective-permute-start | bytes 208904 | tf_op jit(solution)/shard_map/ppermute | solution.py:45
  7.9 5.8 %collective-permute-start = (bf16[48,576]{1,0:T(8,128)(2,1)S(1)}, bf16[48,576]{1,0:T(8,128)(2,1)S(1)}, u32[]{:S(2)}, u32[]{:S(2)}) collective-permute-start(bf16[48,576]{1,0:T(8,128)(2,1)S(1)} %get-tuple-element.17.first_ref), channel_id=1, source_target_pairs={{0,8},{4,12},{8,0},{12,4},{1,9},{5,13},{9,1},{13,5},{2,10},{6,14},... | collective-permute-start | bytes 165896 | tf_op jit(solution)/shard_map/ppermute | solution.py:45
  13.7 6.2 %slice-start = ((s8[7340032]{0:T(1024)(128)(4,1)}), s8[4194304]{0:T(1024)(128)(4,1)S(1)}, s32[]{:S(2)}) async-start(s8[7340032]{0:T(1024)(128)(4,1)} %bitcast.1), calls=%async_computation | async-start | bytes 8388608
  13.7 6.2 %slice-start.1 = ((s8[7340032]{0:T(1024)(128)(4,1)}), s8[3145728]{0:T(1024)(128)(4,1)S(1)}, s32[]{:S(2)}) async-start(s8[7340032]{0:T(1024)(128)(4,1)} %bitcast.1), calls=%async_computation.1 | async-start | bytes 6291456
  13.7 4.9 %collective-permute-start.1 = (bf16[96,576]{1,0:T(8,128)(2,1)S(1)}, bf16[96,576]{1,0:T(8,128)(2,1)S(1)}, u32[]{:S(2)}, u32[]{:S(2)}) collective-permute-start(bf16[96,576]{1,0:T(8,128)(2,1)S(1)} %shard_map.122), channel_id=1, source_target_pairs={{0,4},{4,0},{8,12},{12,8},{1,5},{5,1},{9,13},{13,9},{2,6},{6,2},{1... | collective-permute-start | bytes 331784 | tf_op jit(solution)/shard_map/ppermute | solution.py:45
  14.6 5.3 %collective-permute-start.4 = (bf16[16,2176]{1,0:T(8,128)(2,1)S(1)}, bf16[16,2176]{1,0:T(8,128)(2,1)S(1)}, u32[]{:S(2)}, u32[]{:S(2)}) collective-permute-start(bf16[16,2176]{1,0:T(8,128)(2,1)S(1)} %merge_parts.1.first_ref), channel_id=1, source_target_pairs={{0,8},{4,12},{8,0},{12,4},{1,9},{5,13},{9,1},{13,5},{2,10},{6,14},... | collective-permute-start | bytes 208904 | tf_op jit(solution)/shard_map/ppermute | solution.py:45
  18.7 5.3 %collective-permute-start.2 = (bf16[144,576]{1,0:T(8,128)(2,1)S(1)}, bf16[144,576]{1,0:T(8,128)(2,1)S(1)}, u32[]{:S(2)}, u32[]{:S(2)}) collective-permute-start(bf16[144,576]{1,0:T(8,128)(2,1)S(1)} %shard_map.123.mine_ref), channel_id=1, source_target_pairs={{0,1},{1,0},{2,3},{3,2},{4,5},{5,4},{6,7},{7,6},{8,9},{9,8},{10,11... | collective-permute-start | bytes 497672 | tf_op jit(solution)/shard_map/ppermute | solution.py:45
  21.2 1.2 %collective-permute-start.5 = (bf16[2,16,448]{2,1,0:T(8,128)(2,1)S(1)}, bf16[2,16,448]{2,1,0:T(8,128)(2,1)S(1)}, u32[]{:S(2)}, u32[]{:S(2)}) collective-permute-start(bf16[2,16,448]{2,1,0:T(8,128)(2,1)S(1)} %get-tuple-element.23), channel_id=1, source_target_pairs={{0,1},{1,0},{2,3},{3,2},{4,5},{5,4},{6,7},{7,6},{8,9},{9,8},{10,11... | collective-permute-start | bytes 86024 | tf_op jit(solution)/shard_map/ppermute | solution.py:45
  22.5 3.8 %collective-permute-start.6 = (bf16[1,16,448]{2,1,0:T(8,128)(2,1)S(1)}, bf16[1,16,448]{2,1,0:T(8,128)(2,1)S(1)}, u32[]{:S(2)}, u32[]{:S(2)}) collective-permute-start(bf16[1,16,448]{2,1,0:T(8,128)(2,1)S(1)} %get-tuple-element.25), channel_id=1, source_target_pairs={{0,2},{2,0},{1,3},{3,1},{4,6},{6,4},{5,7},{7,5},{8,10},{10,8},{9,1... | collective-permute-start | bytes 43016 | tf_op jit(solution)/shard_map/ppermute | solution.py:45
where the time goes:
time: 28.1 us; the launch traced here: 27.9 us
  Pallas kernels  10.9 us (39%)
  starting transfers between devices  10.1 us (36%)
  waiting for transfers between devices  6.27 us (22%)
  between operations  0.71 us (3%)
    ppermute x7, starting transfers between devices, swap(): return lax.ppermute(value, axis, [(i, i ^ step) for i in range(size)])  10.1 us
    ppermute x7, waiting for transfers between devices, swap(): return lax.ppermute(value, axis, [(i, i ^ step) for i in range(size)])  6.27 us
    pallas_call x1, Pallas kernels, step_part(): pl.pallas_call(functools.partial(step_kernel, rate), out_shape=(shape((pa...  4.12 us
    pallas_call x1, Pallas kernels, prompt_front(): pl.pallas_call(functools.partial(front_kernel, rate, group, heads), out_s...  2.09 us
    pallas_call x1, Pallas kernels, prompt_back(): pl.pallas_call(functools.partial(back_kernel, rate, group, heads), out_sh...  1.66 us
    pallas_call x1, Pallas kernels, finish_steps(): pl.pallas_call(functools.partial(finish_kernel, rate, heads, parts), out_...  1.34 us
    pallas_call x2, Pallas kernels, prompt_lift(): pl.pallas_call(functools.partial(lift_kernel, heads), out_shape=pltpu.VME...  1.29 us
  transfers between devices with their start and end apart: 7, of which 5 were waited for; matrix products, arithmetic and copies ran while one was open for 0% of the time, Pallas kernels for 18%

commit v1 on v0

--- a/solution.py
+++ b/solution.py
@@ -133,6 +133,7 @@
         fetch(order_hbm, order_ref),
     ]
     cache_copy = fetch(cache_hbm, cache_ref)
+    value_up_copy = fetch(value_up_hbm, value_up_ref)
 
     query_copy.wait()
     query = query_ref[...].astype(F32)
@@ -150,7 +151,6 @@
             row_ref[lane // LANES, pl.ds(head, pairs, stride=heads), :] = lifted[
                 :, lane : lane + LANES
             ]
-    value_up_copy = fetch(value_up_hbm, value_up_ref)
     prompt_copy = fetch(prompt_hbm, prompt_ref)
     row_parts = [row_ref[index] for index in range(latent // LANES)] + [rope]
     query_rows = jnp.concatenate(row_parts, axis=1).astype(BF16)
@@ -431,12 +431,8 @@
     rate, heads, parts, first_ref, second_ref, weight_ref, keep_ref, give_ref
 ):
     merged, _, _ = merge(rate, first_ref, second_ref, heads)
-    chunk = heads // 2
-    size = chunk * merged[0].shape[1]
-    product = 0.0
-    for index in range(2):
-        rows = jnp.concatenate(merged[index * chunk : (index + 1) * chunk], axis=1)
-        product = product + dot(rows, weight_ref[index * size : (index + 1) * size, :])
+    rows = jnp.concatenate(merged, axis=1)
+    product = dot(rows, weight_ref[...])
     width = product.shape[1] // parts
     upper = lax.axis_index("role") == 1
     for index in range(parts // 2):
@@ -734,8 +730,9 @@
         value_up,
         prompt_query,
     )
+    group = 4 if heads % 16 == 0 else 2 if heads % 8 == 0 else 1
     edge = heads - heads // 4
-    early = edge // 2
+    early = heads // 2
     early_rows = prompt_lift(range(early), prompt_query, key_up)
     late_rows = prompt_lift(range(early, heads), prompt_query, key_up)
     rows = (early_rows, late_rows)
@@ -754,7 +751,7 @@
         keys = move_rows(
             extend_kernel, 2 * keys.shape[0], keys, received, swap(received, "role", 1)
         )
-    front = prompt_front(rate, early, range(edge), rows, keys, key_pos, query_pos, value_up)
+    front = prompt_front(rate, group, range(edge), rows, keys, key_pos, query_pos, value_up)
     keep, give = finish_steps(
         rate, heads, head_size * role_size, running, far_running, out_weight
     )
@@ -764,7 +761,7 @@
         partial = swap(give, "head", step)
     return prompt_back(
         rate,
-        heads - edge,
+        group,
         range(edge, heads),
         steps,
         rows,

time: 28.1 us -> 28.1 us (level)
  transfers between devices with their start and end apart: 7 -> 7, of which waited for: 5 -> 4; matrix products, arithmetic and copies ran while one was open for 0% -> 0% of each run, Pallas kernels for 18% -> 18%
where the time goes in v1:
time: 28.1 us; the launch traced here: 28 us
  Pallas kernels  10.9 us (39%)
  starting transfers between devices  10.1 us (36%)
  waiting for transfers between devices  6.21 us (22%)
  between operations  0.7 us (2%)
    ppermute x7, starting transfers between devices, swap(): return lax.ppermute(value, axis, [(i, i ^ step) for i in range(size)])  10.1 us
    ppermute x7, waiting for transfers between devices, swap(): return lax.ppermute(value, axis, [(i, i ^ step) for i in range(size)])  6.21 us
    pallas_call x1, Pallas kernels, step_part(): pl.pallas_call(functools.partial(step_kernel, rate), out_shape=(shape((pa...  4.12 us
    pallas_call x1, Pallas kernels, prompt_front(): pl.pallas_call(functools.partial(front_kernel, rate, group, heads), out_s...  2.22 us
    pallas_call x1, Pallas kernels, prompt_back(): pl.pallas_call(functools.partial(back_kernel, rate, group, heads), out_sh...  1.66 us
    pallas_call x1, Pallas kernels, finish_steps(): pl.pallas_call(functools.partial(finish_kernel, rate, heads, parts), out_...  1.34 us
    pallas_call x2, Pallas kernels, prompt_lift(): pl.pallas_call(functools.partial(lift_kernel, heads), out_shape=pltpu.VME...  1.23 us
  transfers between devices with their start and end apart: 7, of which 4 were waited for; matrix products, arithmetic and copies ran while one was open for 0% of the time, Pallas kernels for 18%

profile of v1, /device:TPU:0, one launch (start us, length us, event | category | flops | bytes accessed | tf_op | source)
XLA Modules:
  0.0 28.0 jit_solution(3710539753681311567)
XLA Ops:
  0.6 4.1 %step_part.1 = (bf16[16,2176]{1,0:T(8,128)(2,1)S(1)}, bf16[16,128,512]{2,1,0:T(8,128)(2,1)S(1)}, bf16[16,512,128]{2,1,0:T(8,128)(2,1)S(1)}, bf16[96,576]{1,0:T(8...) custom-call(s32[4]{0:T(128)} %order_hbm.1, ...), custom_call_target="tpu_custom_call" | custom-call | flops 1000000000 | bytes 10000000 | tf_op jit(solution)/shard_map/step_part/pallas_call | solution.py:270
  4.8 3.1 %collective-permute-start.3 = (bf16[16,2176]{1,0:T(8,128)(2,1)S(1)}, bf16[16,2176]{1,0:T(8,128)(2,1)S(1)}, u32[]{:S(2)}, u32[]{:S(2)}) collective-permute-start(bf16[16,2176]{1,0:T(8,128)(2,1)S(1)} %get-tuple-element.21.first_ref), channel_id=1, source_target_pairs={{0,4},{4,0},{8,12},{12,8},{1,5},{5,1},{9,13},{13,9},{2,6},{6,2},{1... | collective-permute-start | bytes 208904 | tf_op jit(solution)/shard_map/ppermute | solution.py:45
  7.9 2.6 %collective-permute-start = (bf16[48,576]{1,0:T(8,128)(2,1)S(1)}, bf16[48,576]{1,0:T(8,128)(2,1)S(1)}, u32[]{:S(2)}, u32[]{:S(2)}) collective-permute-start(bf16[48,576]{1,0:T(8,128)(2,1)S(1)} %get-tuple-element.17.first_ref), channel_id=1, source_target_pairs={{0,8},{4,12},{8,0},{12,4},{1,9},{5,13},{9,1},{13,5},{2,10},{6,14},... | collective-permute-start | bytes 165896 | tf_op jit(solution)/shard_map/ppermute | solution.py:45
  10.5 3.2 %collective-permute-done.second_ref.first_ref = bf16[48,576]{1,0:T(8,128)(2,1)S(1)} collective-permute-done((bf16[48,576]{1,0:T(8,128)(2,1)S(1)}, bf16[48,576]{1,0:T(8,128)(2,1)S(1)}, u32[]{:S(2)}, u32[]{:S(2)}) %collective-permute-start) | collective-permute-done | bytes 55328 | tf_op jit(solution)/shard_map/ppermute | solution.py:45
  13.7 0.0 slice-start
  13.7 0.0 slice-start.1
  13.7 0.6 %collective-permute-start.1 = (bf16[96,576]{1,0:T(8,128)(2,1)S(1)}, bf16[96,576]{1,0:T(8,128)(2,1)S(1)}, u32[]{:S(2)}, u32[]{:S(2)}) collective-permute-start(bf16[96,576]{1,0:T(8,128)(2,1)S(1)} %shard_map.122), channel_id=1, source_target_pairs={{0,4},{4,0},{8,12},{12,8},{1,5},{5,1},{9,13},{13,9},{2,6},{6,2},{1... | collective-permute-start | bytes 331784 | tf_op jit(solution)/shard_map/ppermute | solution.py:45
  14.3 0.0 collective-permute-done.3.second_ref
  14.3 0.3 merge_parts.1.first_ref
  14.6 2.1 %collective-permute-start.4 = (bf16[16,2176]{1,0:T(8,128)(2,1)S(1)}, bf16[16,2176]{1,0:T(8,128)(2,1)S(1)}, u32[]{:S(2)}, u32[]{:S(2)}) collective-permute-start(bf16[16,2176]{1,0:T(8,128)(2,1)S(1)} %merge_parts.1.first_ref), channel_id=1, source_target_pairs={{0,8},{4,12},{8,0},{12,4},{1,9},{5,13},{9,1},{13,5},{2,10},{6,14},... | collective-permute-start | bytes 208904 | tf_op jit(solution)/shard_map/ppermute | solution.py:45
  16.7 2.0 %collective-permute-done.1.second_ref = bf16[96,576]{1,0:T(8,128)(2,1)S(1)} collective-permute-done((bf16[96,576]{1,0:T(8,128)(2,1)S(1)}, bf16[96,576]{1,0:T(8,128)(2,1)S(1)}, u32[]{:S(2)}, u32[]{:S(2)}) %collective-permute-start.1) | collective-permute-done | bytes 110624 | tf_op jit(solution)/shard_map/ppermute | solution.py:45
  18.7 0.1 collective-permute-start.2
  18.8 0.6 %prompt_lift.2.early_ref = bf16[768,576]{1,0:T(8,128)(2,1)S(1)} custom-call(bf16[96,16,192]{2,1,0:T(8,128)(2,1)S(1)} %get-tuple-element.14.query_ref, bf16[16,128,512]{2,1,0:T(8,128)(2,1)S(1)} %get-tuple-element.15.key_up_ref), custom_call_target="tpu_custom_call" | custom-call | flops 800000000 | bytes 3000000 | tf_op jit(solution)/shard_map/prompt_lift/pallas_call | solution.py:501
  19.4 0.5 %collective-permute-done.4.second_ref = bf16[16,2176]{1,0:T(8,128)(2,1)S(1)} collective-permute-done((bf16[16,2176]{1,0:T(8,128)(2,1)S(1)}, bf16[16,2176]{1,0:T(8,128)(2,1)S(1)}, u32[]{:S(2)}, u32[]{:S(2)}) %collective-permute-start.4) | collective-permute-done | bytes 69664 | tf_op jit(solution)/shard_map/ppermute | solution.py:45
  19.9 0.0 slice-done
  19.9 0.0 slice-done.1
  19.9 1.3 %finish_steps.1 = (f32[2,16,448]{2,1,0:T(8,128)S(1)}, bf16[2,16,448]{2,1,0:T(8,128)(2,1)S(1)}) custom-call(bf16[16,2176]{1,0:T(8,128)(2,1)S(1)} %merge_parts.1.first_ref, bf16[16,2176]{1,0:T(8,128)(2,1)S(1)} %collective-permute-done.4.second_ref, bf16[2048,1792]{1,0:T(8,128)(2,1)S(1)} %bitcast.2), custom_call_target="tpu_custom_call" | custom-call | flops 500000000 | bytes 8000000 | tf_op jit(solution)/shard_map/finish_steps/pallas_call | solution.py:449
  21.2 0.1 collective-permute-start.5
  21.3 0.6 %prompt_lift.3.late_ref = bf16[768,576]{1,0:T(8,128)(2,1)S(1)} custom-call(bf16[96,16,192]{2,1,0:T(8,128)(2,1)S(1)} %get-tuple-element.14.query_ref, bf16[16,128,512]{2,1,0:T(8,128)(2,1)S(1)} %get-tuple-element.15.key_up_ref), custom_call_target="tpu_custom_call" | custom-call | flops 800000000 | bytes 3000000 | tf_op jit(solution)/shard_map/prompt_lift/pallas_call | solution.py:501
  21.9 0.5 %collective-permute-done.5.received_ref = bf16[2,16,448]{2,1,0:T(8,128)(2,1)S(1)} collective-permute-done((bf16[2,16,448]{2,1,0:T(8,128)(2,1)S(1)}, bf16[2,16,448]{2,1,0:T(8,128)(2,1)S(1)}, u32[]{:S(2)}, u32[]{:S(2)}) %collective-permute-start.5) | collective-permute-done | bytes 28704 | tf_op jit(solution)/shard_map/ppermute | solution.py:45
  22.5 1.6 %collective-permute-start.6 = (bf16[1,16,448]{2,1,0:T(8,128)(2,1)S(1)}, bf16[1,16,448]{2,1,0:T(8,128)(2,1)S(1)}, u32[]{:S(2)}, u32[]{:S(2)}) collective-permute-start(bf16[1,16,448]{2,1,0:T(8,128)(2,1)S(1)} %get-tuple-element.25), channel_id=1, source_target_pairs={{0,2},{2,0},{1,3},{3,1},{4,6},{6,4},{5,7},{7,5},{8,10},{10,8},{9,1... | collective-permute-start | bytes 43016 | tf_op jit(solution)/shard_map/ppermute | solution.py:45
  24.0 0.0 collective-permute-done.2.other_ref
  24.1 2.2 %prompt_front.1.front_ref = bf16[96,1536]{1,0:T(8,128)(2,1)S(1)} custom-call(bf16[768,576]{1,0:T(8,128)(2,1)S(1)} %prompt_lift.2.early_ref, bf16[768,576]{1,0:T(8,128)(2,1)S(1)} %prompt_lift.3.late_ref, bf16[384,576]{1,0:T(8,128)(2,1)S(1)} %shard_map.124.key_ref, s32[8,384]{1,0:T(8,128)S(1)} %get-tuple-element.18.key_pos_ref, ...), custom_call_target="tpu_custom_call" | custom-call | flops 400000000 | bytes 3000000 | tf_op jit(solution)/shard_map/prompt_front/pallas_call | solution.py:583
  26.3 0.0 collective-permute-done.6.received_ref
  26.3 1.7 %prompt_back.1 = (bf16[96,2048]{1,0:T(8,128)(2,1)}, bf16[4,4,448]{2,1,0:T(4,128)(2,1)}) custom-call(bf16[768,576]{1,0:T(8,128)(2,1)S(1)} %prompt_lift.2.early_ref, bf16[768,576]{1,0:T(8,128)(2,1)S(1)} %prompt_lift.3.late_ref, bf16[384,576]{1,0:T(8,128)(2,1)S(1)} %shard_map.124.key_ref, s32[8,384]{1,0:T(8,128)S(1)} %get-tuple-element.18.key_pos_ref, ...), custom_call_target="tpu_custom_call" | custom-call | flops 800000000 | bytes 6000000 | tf_op jit(solution)/shard_map/prompt_back/pallas_call | solution.py:663
  (5 shorter events, 0.1 us)
Async XLA Ops:
  4.8 9.6 %collective-permute-start.3 = (bf16[16,2176]{1,0:T(8,128)(2,1)S(1)}, bf16[16,2176]{1,0:T(8,128)(2,1)S(1)}, u32[]{:S(2)}, u32[]{:S(2)}) collective-permute-start(bf16[16,2176]{1,0:T(8,128)(2,1)S(1)} %get-tuple-element.21.first_ref), channel_id=1, source_target_pairs={{0,4},{4,0},{8,12},{12,8},{1,5},{5,1},{9,13},{13,9},{2,6},{6,2},{1... | collective-permute-start | bytes 208904 | tf_op jit(solution)/shard_map/ppermute | solution.py:45
  7.9 5.8 %collective-permute-start = (bf16[48,576]{1,0:T(8,128)(2,1)S(1)}, bf16[48,576]{1,0:T(8,128)(2,1)S(1)}, u32[]{:S(2)}, u32[]{:S(2)}) collective-permute-start(bf16[48,576]{1,0:T(8,128)(2,1)S(1)} %get-tuple-element.17.first_ref), channel_id=1, source_target_pairs={{0,8},{4,12},{8,0},{12,4},{1,9},{5,13},{9,1},{13,5},{2,10},{6,14},... | collective-permute-start | bytes 165896 | tf_op jit(solution)/shard_map/ppermute | solution.py:45
  13.7 6.2 %slice-start = ((s8[7340032]{0:T(1024)(128)(4,1)}), s8[4194304]{0:T(1024)(128)(4,1)S(1)}, s32[]{:S(2)}) async-start(s8[7340032]{0:T(1024)(128)(4,1)} %bitcast.1), calls=%async_computation | async-start | bytes 8388608
  13.7 6.2 %slice-start.1 = ((s8[7340032]{0:T(1024)(128)(4,1)}), s8[3145728]{0:T(1024)(128)(4,1)S(1)}, s32[]{:S(2)}) async-start(s8[7340032]{0:T(1024)(128)(4,1)} %bitcast.1), calls=%async_computation.1 | async-start | bytes 6291456
  13.7 4.9 %collective-permute-start.1 = (bf16[96,576]{1,0:T(8,128)(2,1)S(1)}, bf16[96,576]{1,0:T(8,128)(2,1)S(1)}, u32[]{:S(2)}, u32[]{:S(2)}) collective-permute-start(bf16[96,576]{1,0:T(8,128)(2,1)S(1)} %shard_map.122), channel_id=1, source_target_pairs={{0,4},{4,0},{8,12},{12,8},{1,5},{5,1},{9,13},{13,9},{2,6},{6,2},{1... | collective-permute-start | bytes 331784 | tf_op jit(solution)/shard_map/ppermute | solution.py:45
  14.6 5.3 %collective-permute-start.4 = (bf16[16,2176]{1,0:T(8,128)(2,1)S(1)}, bf16[16,2176]{1,0:T(8,128)(2,1)S(1)}, u32[]{:S(2)}, u32[]{:S(2)}) collective-permute-start(bf16[16,2176]{1,0:T(8,128)(2,1)S(1)} %merge_parts.1.first_ref), channel_id=1, source_target_pairs={{0,8},{4,12},{8,0},{12,4},{1,9},{5,13},{9,1},{13,5},{2,10},{6,14},... | collective-permute-start | bytes 208904 | tf_op jit(solution)/shard_map/ppermute | solution.py:45
  18.7 5.3 %collective-permute-start.2 = (bf16[144,576]{1,0:T(8,128)(2,1)S(1)}, bf16[144,576]{1,0:T(8,128)(2,1)S(1)}, u32[]{:S(2)}, u32[]{:S(2)}) collective-permute-start(bf16[144,576]{1,0:T(8,128)(2,1)S(1)} %shard_map.123.mine_ref), channel_id=1, source_target_pairs={{0,1},{1,0},{2,3},{3,2},{4,5},{5,4},{6,7},{7,6},{8,9},{9,8},{10,11... | collective-permute-start | bytes 497672 | tf_op jit(solution)/shard_map/ppermute | solution.py:45
  21.2 1.2 %collective-permute-start.5 = (bf16[2,16,448]{2,1,0:T(8,128)(2,1)S(1)}, bf16[2,16,448]{2,1,0:T(8,128)(2,1)S(1)}, u32[]{:S(2)}, u32[]{:S(2)}) collective-permute-start(bf16[2,16,448]{2,1,0:T(8,128)(2,1)S(1)} %get-tuple-element.23), channel_id=1, source_target_pairs={{0,1},{1,0},{2,3},{3,2},{4,5},{5,4},{6,7},{7,6},{8,9},{9,8},{10,11... | collective-permute-start | bytes 86024 | tf_op jit(solution)/shard_map/ppermute | solution.py:45
  22.5 3.8 %collective-permute-start.6 = (bf16[1,16,448]{2,1,0:T(8,128)(2,1)S(1)}, bf16[1,16,448]{2,1,0:T(8,128)(2,1)S(1)}, u32[]{:S(2)}, u32[]{:S(2)}) collective-permute-start(bf16[1,16,448]{2,1,0:T(8,128)(2,1)S(1)} %get-tuple-element.25), channel_id=1, source_target_pairs={{0,2},{2,0},{1,3},{3,1},{4,6},{6,4},{5,7},{7,5},{8,10},{10,8},{9,1... | collective-permute-start | bytes 43016 | tf_op jit(solution)/shard_map/ppermute | solution.py:45
